TPU v7x, 32 devices: a whole 2x2x4 slice. The times are simulated.
32 devices in a mesh: outer: 4 (over y, x), inner: 8 (over z, core).
Axes of the slice: x: 2, y: 2, z: 4, core: 2. Of those that a mesh axis runs over, the one named last changes fastest.
Arguments:
- queries: bfloat16 [8192, 1024], P(('outer', 'inner')), may hold values from -480 to 480
- keys: bfloat16 [8192, 512], P(('outer', 'inner')), may hold values from -8 to 8
- values: bfloat16 [8192, 512], P(('outer', 'inner')), may hold values from -4 to 4
- residual: bfloat16 [8192, 1024], P(('outer', 'inner')), may hold values from -5 to 5
- norm_gain: float32 [1024], replicated, may hold values from 0.1 to 1.9
- w_gate: bfloat16 [8, 1024, 512], P('inner'), may hold values from -0.1875 to 0.1875
- w_up: bfloat16 [8, 1024, 512], P('inner'), may hold values from -0.1875 to 0.1875
- w_down: bfloat16 [8, 512, 1024], P('inner'), may hold values from -0.25 to 0.25
- routes: int32 [8192, 2], P(('outer', 'inner')), may hold values from 0 to 7, all different within a row; in each aligned block of 256 rows (0 to 255, 256 to 511, ...) at most 128 rows name the same one
- gates: float32 [8192, 2], P(('outer', 'inner')), may hold values from 0.2 to 1
Outputs:
- layer_out: bfloat16 [8192, 1024], P(('outer', 'inner'))
Inputs may be any that keep to these rules, and one draw needn't show every extreme that they name: `routes`: A patch's two experts differ. Within one block of 256 patches no expert is picked more than 128 times, and in some block one expert is picked exactly 128 times.
All inputs are finite; a program needn't handle non-finite values.
Results may differ from a plain program's by a relative error of at most 0.0085.
Values may be sent and summed in bfloat16 or wider, within the bound.
A program may use at most 64 MiB of HBM per device.

v0:
```python
import math

import jax
import jax.numpy as jnp
from jax import lax
from jax.sharding import PartitionSpec as P

D = 1024
QH = 8
KVH = 4
DH = 128
BACK = 3


def shifted(value, axis, steps):
    count = lax.axis_size(axis)
    first, last = (max(0, -steps), min(count, count - steps))
    return lax.ppermute(value, axis, [(source, source + steps) for source in range(first, last)])


def feed_forward(rows, gate_matrix, up_matrix, down_matrix):
    gate_part = jnp.dot(rows, gate_matrix, preferred_element_type=jnp.float32)
    up_part = jnp.dot(rows, up_matrix, preferred_element_type=jnp.float32)
    inner_act = (jax.nn.silu(gate_part) * up_part).astype(jnp.bfloat16)
    return jnp.dot(inner_act, down_matrix, preferred_element_type=jnp.float32).astype(jnp.bfloat16)


def local(queries, keys, values, residual, norm_gain, w_gate, w_up, w_down, routes, gates):
    tok_rows = queries.shape[0]
    groups = QH // KVH
    device_index = lax.axis_index(("outer", "inner"))
    current = (keys, values)
    earlier = []
    for step_index in range(BACK):
        current = shifted((current[0], current[1]), ("outer", "inner"), 1)
        earlier = [current] + earlier
    key_window = jnp.concatenate([block_pair[0] for block_pair in earlier] + [keys], 0)
    value_window = jnp.concatenate([block_pair[1] for block_pair in earlier] + [values], 0)
    window_rows = key_window.shape[0]
    query_heads = queries.reshape(tok_rows, KVH, groups, DH)
    key_heads = key_window.reshape(window_rows, KVH, DH)
    value_heads = value_window.reshape(window_rows, KVH, DH)
    scores = jnp.einsum(
        "tkgd,skd->kgts", query_heads, key_heads, preferred_element_type=jnp.float32
    ) * (1.0 / math.sqrt(DH))
    query_pos = device_index * tok_rows + jnp.arange(tok_rows, dtype=jnp.int32)
    key_pos = (device_index - BACK) * tok_rows + jnp.arange(window_rows, dtype=jnp.int32)
    allowed = (key_pos[None, :] >= 0) & (key_pos[None, :] <= query_pos[:, None])
    scores = jnp.where(allowed, scores, -jnp.inf)
    highest = jnp.max(scores, -1, keepdims=True)
    expd = jnp.exp(scores - highest)
    weights = (expd / jnp.sum(expd, -1, keepdims=True)).astype(jnp.bfloat16)
    mixed = jnp.einsum("kgts,skd->tkgd", weights, value_heads, preferred_element_type=jnp.float32)
    attended = mixed.astype(jnp.bfloat16).reshape(tok_rows, QH * DH)
    stream = residual.astype(jnp.float32) + attended.astype(jnp.float32)
    mean_sq = jnp.mean(stream * stream, -1, keepdims=True)
    normed = (stream * lax.rsqrt(mean_sq + 1e-06) * norm_gain).astype(jnp.bfloat16)
    owners = lax.axis_size("inner")
    capacity = 4 * tok_rows // owners
    picks = routes.reshape(-1)
    one_hot = (picks[:, None] == jnp.arange(owners, dtype=jnp.int32)[None, :]).astype(jnp.int32)
    order_rank = jnp.sum((jnp.cumsum(one_hot, 0) - 1) * one_hot, 1)
    slot_index = picks * capacity + order_rank
    slot_pair = slot_index.reshape(tok_rows, 2)
    slot_grid = jnp.arange(owners * capacity, dtype=jnp.int32)[:, None]
    placing = ((slot_pair[None, :, 0] == slot_grid) | (slot_pair[None, :, 1] == slot_grid)).astype(
        jnp.bfloat16
    )
    outgoing = (
        jnp.dot(placing, normed, preferred_element_type=jnp.float32)
        .astype(jnp.bfloat16)
        .reshape(owners, capacity, D)
    )
    gate_matrix = w_gate[0]
    up_matrix = w_up[0]
    down_matrix = w_down[0]
    arrived = lax.all_to_all(outgoing, "inner", split_axis=0, concat_axis=0, tiled=True)
    results = feed_forward(arrived.reshape(-1, D), gate_matrix, up_matrix, down_matrix).reshape(
        arrived.shape
    )
    returned = lax.all_to_all(results, "inner", split_axis=0, concat_axis=0, tiled=True)
    picked = (
        returned.reshape(owners * capacity, D)[slot_index]
        .astype(jnp.float32)
        .reshape(tok_rows, 2, D)
    )
    mixture = jnp.sum(gates[:, :, None] * picked, 1)
    return (stream + mixture).astype(jnp.bfloat16)


def solution(mesh):
    return jax.shard_map(
        local,
        mesh=mesh,
        in_specs=(
            P(("outer", "inner"), None),
            P(("outer", "inner"), None),
            P(("outer", "inner"), None),
            P(("outer", "inner"), None),
            P(),
            P("inner", None, None),
            P("inner", None, None),
            P("inner", None, None),
            P(("outer", "inner"), None),
            P(("outer", "inner"), None),
        ),
        out_specs=P(("outer", "inner"), None),
        check_vma=False,
    )
```

profile of v0, /device:TPU:4, one launch (start us, length us, event | category | flops | bytes accessed | tf_op | source)
XLA Modules:
  0.0 177.8 jit_solution(39388173408413153)
XLA Ops:
  0.0 1.2 copy.28
  1.2 1.9 %collective-permute-start.3 = (bf16[256,512]{0,1:T(8,128)(2,1)S(1)}, bf16[256,512]{0,1:T(8,128)(2,1)S(1)}, u32[]{:S(2)}, u32[]{:S(2)}) collective-permute-start(bf16[256,512]{0,1:T(8,128)(2,1)S(1)} %copy.28), channel_id=1, source_target_pairs={{0,1},{1,2},{2,3},{3,4},{4,5},{5,6},{6,7},{7,8},{8,9},{9,10},{10,1... | collective-permute-start | bytes 786440 | tf_op jit(solution)/shard_map/ppermute | solution.py:18
  3.1 3.6 %collective-permute-start = (bf16[256,512]{1,0:T(8,128)(2,1)}, bf16[256,512]{1,0:T(8,128)(2,1)S(1)}, u32[]{:S(2)}, u32[]{:S(2)}) collective-permute-start(bf16[256,512]{1,0:T(8,128)(2,1)} %param.12), channel_id=1, source_target_pairs={{0,1},{1,2},{2,3},{3,4},{4,5},{5,6},{6,7},{7,8},{8,9},{9,10},{10,1... | collective-permute-start | bytes 786440 | tf_op jit(solution)/shard_map/ppermute | solution.py:18
  9.4 3.1 %collective-permute-done.3 = bf16[256,512]{0,1:T(8,128)(2,1)S(1)} collective-permute-done((bf16[256,512]{0,1:T(8,128)(2,1)S(1)}, bf16[256,512]{0,1:T(8,128)(2,1)S(1)}, u32[]{:S(2)}, u32[]{:S(2)}) %collective-permute-start.3) | collective-permute-done | bytes 262176 | tf_op jit(solution)/shard_map/ppermute | solution.py:18
  12.5 1.9 %collective-permute-start.4 = (bf16[256,512]{0,1:T(8,128)(2,1)S(1)}, bf16[256,512]{0,1:T(8,128)(2,1)}, u32[]{:S(2)}, u32[]{:S(2)}) collective-permute-start(bf16[256,512]{0,1:T(8,128)(2,1)S(1)} %collective-permute-done.3), channel_id=1, source_target_pairs={{0,1},{1,2},{2,3},{3,4},{4,5},{5,6},{6,7},{7,8},{8,9},{9,10},{10,1... | collective-permute-start | bytes 786440 | tf_op jit(solution)/shard_map/ppermute | solution.py:18
  15.3 1.9 %collective-permute-start.1 = (bf16[256,512]{1,0:T(8,128)(2,1)S(1)}, bf16[256,512]{1,0:T(8,128)(2,1)S(1)}, u32[]{:S(2)}, u32[]{:S(2)}) collective-permute-start(bf16[256,512]{1,0:T(8,128)(2,1)S(1)} %collective-permute-done), channel_id=1, source_target_pairs={{0,1},{1,2},{2,3},{3,4},{4,5},{5,6},{6,7},{7,8},{8,9},{9,10},{10,1... | collective-permute-start | bytes 786440 | tf_op jit(solution)/shard_map/ppermute | solution.py:18
  17.4 6.5 %collective-permute-done.4 = bf16[256,512]{0,1:T(8,128)(2,1)} collective-permute-done((bf16[256,512]{0,1:T(8,128)(2,1)S(1)}, bf16[256,512]{0,1:T(8,128)(2,1)}, u32[]{:S(2)}, u32[]{:S(2)}) %collective-permute-start.4) | collective-permute-done | bytes 262176 | tf_op jit(solution)/shard_map/ppermute | solution.py:18
  23.9 1.9 %collective-permute-start.5 = (bf16[256,512]{0,1:T(8,128)(2,1)}, bf16[256,512]{0,1:T(8,128)(2,1)}, u32[]{:S(2)}, u32[]{:S(2)}) collective-permute-start(bf16[256,512]{0,1:T(8,128)(2,1)} %collective-permute-done.4), channel_id=1, source_target_pairs={{0,1},{1,2},{2,3},{3,4},{4,5},{5,6},{6,7},{7,8},{8,9},{9,10},{10,1... | collective-permute-start | bytes 786440 | tf_op jit(solution)/shard_map/ppermute | solution.py:18
  26.6 1.9 %collective-permute-start.2 = (bf16[256,512]{1,0:T(8,128)(2,1)S(1)}, bf16[256,512]{1,0:T(8,128)(2,1)}, u32[]{:S(2)}, u32[]{:S(2)}) collective-permute-start(bf16[256,512]{1,0:T(8,128)(2,1)S(1)} %collective-permute-done.1), channel_id=1, source_target_pairs={{0,1},{1,2},{2,3},{3,4},{4,5},{5,6},{6,7},{7,8},{8,9},{9,10},{10,1... | collective-permute-start | bytes 786440 | tf_op jit(solution)/shard_map/ppermute | solution.py:18
  29.6 1.2 reshape.106
  30.9 7.3 %collective-permute-done.2 = bf16[256,512]{1,0:T(8,128)(2,1)} collective-permute-done((bf16[256,512]{1,0:T(8,128)(2,1)S(1)}, bf16[256,512]{1,0:T(8,128)(2,1)}, u32[]{:S(2)}, u32[]{:S(2)}) %collective-permute-start.2) | collective-permute-done | bytes 262176 | tf_op jit(solution)/shard_map/ppermute | solution.py:18
  38.3 1.3 pad_maximum_fusion
  40.1 1.2 pad_maximum_fusion.1
  41.3 7.1 %fusion.35 = (f32[4,2,256]{2,1,0:T(2,128)S(1)}, f32[4,2,256,1024]{2,3,1,0:T(8,128)}) fusion(pred[256,1024]{0,1:T(8,128)(4,1)} %compare_and_fusion, bf16[1024,4,128,1]{0,2,3,1:T(8,128)(2,1)S(1)} %bitcast.57, bf16[256,4,2,128]{3,2,1,0:T(2,128)(2,1)} %reshape.106), kind=kOutput, calls=%fused_computation.58 | convolution fusion | flops 545260544 | bytes 10231808 | tf_op jit(solution)/shard_map/sub | solution.py:51
  48.5 5.2 %fusion.7 = f32[4,128,2,256]{3,1,2,0:T(8,128)} fusion(bf16[1024,4,128,1]{0,2,3,1:T(8,128)(2,1)S(1)} %bitcast.56, f32[4,2,256,1024]{2,3,1,0:T(8,128)} %get-tuple-element.10, f32[4,2,256]{2,1,0:T(2,128)S(1)} %get-tuple-element.9), kind=kOutput, calls=%fused_computation.15 | convolution fusion | flops 541589504 | bytes 10493952 | tf_op jit(solution)/shard_map/kgts,skd->tkgd/dot_general | solution.py:53
  53.6 1.6 copy.33
  56.4 51.6 %all_to_all.10 = bf16[8,128,1024]{2,1,0:T(8,128)(2,1)S(1)} all-to-all(bf16[8,128,1024]{2,1,0:T(8,128)(2,1)S(1)} %bitcast.52), channel_id=1, replica_groups=mesh['outer'=4,'inner'=8] {'inner'}, dimensions={0} | all-to-all | bytes 4194304 | tf_op jit(solution)/shard_map/all_to_all | solution.py:77
  108.0 2.6 %fusion.11 = f32[1024,512]{1,0:T(8,128)} fusion(bf16[1024,1024]{1,0:T(8,128)(2,1)S(1)} %bitcast.54, bf16[1,1024,512]{2,1,0:T(8,128)(2,1)S(1)} %copy-done.11), kind=kOutput, calls=%fused_computation.20 | convolution fusion | flops 1073741824 | bytes 5242880 | tf_op jit(solution)/shard_map/dot_general | solution.py:22
  110.6 5.6 %convolution_convert_fusion = bf16[1024,1024]{1,0:T(8,128)(2,1)} fusion(f32[1024,512]{1,0:T(8,128)} %fusion.11, bf16[1024,1024]{1,0:T(8,128)(2,1)S(1)} %bitcast.55, bf16[1,512,1024]{2,1,0:T(8,128)(2,1)S(1)} %copy-done, bf16[1,1024,512]{2,1,0:T(8,128)(2,1)} %param.16), kind=kOutput, calls=%fused_computation.12 | convolution fusion | flops 2151677952 | bytes 8388608 | tf_op jit(solution)/shard_map/dot_general | solution.py:25
  116.2 3.9 %all-to-all-start.1 = ((bf16[8,128,1024]{2,1,0:T(8,128)(2,1)}), bf16[8,128,1024]{2,1,0:T(8,128)(2,1)S(1)}, u32[]{:S(2)}, u32[]{:S(2)}) async-start(bf16[8,128,1024]{2,1,0:T(8,128)(2,1)} %bitcast.53), calls=%async_computation.1 | async-start | bytes 4194304 | tf_op jit(solution)/shard_map/all_to_all | solution.py:81
  120.5 48.5 %all-to-all-done.1 = bf16[8,128,1024]{2,1,0:T(8,128)(2,1)S(1)} async-done(((bf16[8,128,1024]{2,1,0:T(8,128)(2,1)}), bf16[8,128,1024]{2,1,0:T(8,128)(2,1)S(1)}, u32[]{:S(2)}, u32[]{:S(2)}) %all-to-all-start.1) | async-done | bytes 2097184 | tf_op jit(solution)/shard_map/all_to_all | solution.py:81
  168.9 2.8 %gather_fusion = bf16[512,1024]{1,0:T(8,128)(2,1)} fusion(bf16[1024,1024]{1,0:T(8,128)(2,1)S(1)} %bitcast.51, s32[1024]{0:T(1024)S(1)} %pad_clamp_fusion), kind=kCustom, calls=%fused_computation | custom fusion | bytes 2099200 | tf_op jit(solution)/shard_map/gather | solution.py:83
  171.7 2.4 %reshape.113 = f32[256,2,1024]{2,1,0:T(2,128)S(1)} reshape(bf16[512,1024]{1,0:T(8,128)(2,1)} %gather_fusion) | data formatting | bytes 3145728 | tf_op jit(solution)/shard_map/convert_element_type | solution.py:84
  174.1 2.6 %multiply_reduce_fusion = f32[256,1024]{1,0:T(8,128)S(1)} fusion(f32[256,2,1024]{2,1,0:T(2,128)S(1)} %reshape.113, f32[256,2]{1,0:T(8,128)S(1)} %copy.34), kind=kLoop, calls=%fused_computation.10 | loop fusion | flops 786432 | bytes 3147776 | tf_op jit(solution)/shard_map/reduce_sum | solution.py:87
  (52 shorter events, 8.7 us)
Async XLA Ops:
  0.0 110.6 %copy-start = (bf16[1,512,1024]{2,1,0:T(8,128)(2,1)S(1)}, bf16[1,512,1024]{2,1,0:T(8,128)(2,1)}, u32[]{:S(2)}) copy-start(bf16[1,512,1024]{2,1,0:T(8,128)(2,1)} %param.17) | copy-start | bytes 3145732
  0.0 29.6 %copy-start.5 = (bf16[256,1024]{1,0:T(8,128)(2,1)S(1)}, bf16[256,1024]{1,0:T(8,128)(2,1)}, u32[]{:S(2)}) copy-start(bf16[256,1024]{1,0:T(8,128)(2,1)} %param.10) | copy-start | bytes 1572868
  1.2 11.3 %collective-permute-start.3 = (bf16[256,512]{0,1:T(8,128)(2,1)S(1)}, bf16[256,512]{0,1:T(8,128)(2,1)S(1)}, u32[]{:S(2)}, u32[]{:S(2)}) collective-permute-start(bf16[256,512]{0,1:T(8,128)(2,1)S(1)} %copy.28), channel_id=1, source_target_pairs={{0,1},{1,2},{2,3},{3,4},{4,5},{5,6},{6,7},{7,8},{8,9},{9,10},{10,1... | collective-permute-start | bytes 786440 | tf_op jit(solution)/shard_map/ppermute | solution.py:18
  3.1 12.2 %collective-permute-start = (bf16[256,512]{1,0:T(8,128)(2,1)}, bf16[256,512]{1,0:T(8,128)(2,1)S(1)}, u32[]{:S(2)}, u32[]{:S(2)}) collective-permute-start(bf16[256,512]{1,0:T(8,128)(2,1)} %param.12), channel_id=1, source_target_pairs={{0,1},{1,2},{2,3},{3,4},{4,5},{5,6},{6,7},{7,8},{8,9},{9,10},{10,1... | collective-permute-start | bytes 786440 | tf_op jit(solution)/shard_map/ppermute | solution.py:18
  12.5 18.4 %copy-start.6 = (bf16[256,512]{0,1:T(8,128)(2,1)}, bf16[256,512]{0,1:T(8,128)(2,1)S(1)}, u32[]{:S(2)}) copy-start(bf16[256,512]{0,1:T(8,128)(2,1)S(1)} %collective-permute-done.3) | copy-start | bytes 786436
  12.5 11.4 %collective-permute-start.4 = (bf16[256,512]{0,1:T(8,128)(2,1)S(1)}, bf16[256,512]{0,1:T(8,128)(2,1)}, u32[]{:S(2)}, u32[]{:S(2)}) collective-permute-start(bf16[256,512]{0,1:T(8,128)(2,1)S(1)} %collective-permute-done.3), channel_id=1, source_target_pairs={{0,1},{1,2},{2,3},{3,4},{4,5},{5,6},{6,7},{7,8},{8,9},{9,10},{10,1... | collective-permute-start | bytes 786440 | tf_op jit(solution)/shard_map/ppermute | solution.py:18
  15.3 15.6 %copy-start.7 = (bf16[256,512]{1,0:T(8,128)(2,1)}, bf16[256,512]{1,0:T(8,128)(2,1)S(1)}, u32[]{:S(2)}) copy-start(bf16[256,512]{1,0:T(8,128)(2,1)S(1)} %collective-permute-done) | copy-start | bytes 786436
  15.3 11.3 %collective-permute-start.1 = (bf16[256,512]{1,0:T(8,128)(2,1)S(1)}, bf16[256,512]{1,0:T(8,128)(2,1)S(1)}, u32[]{:S(2)}, u32[]{:S(2)}) collective-permute-start(bf16[256,512]{1,0:T(8,128)(2,1)S(1)} %collective-permute-done), channel_id=1, source_target_pairs={{0,1},{1,2},{2,3},{3,4},{4,5},{5,6},{6,7},{7,8},{8,9},{9,10},{10,1... | collective-permute-start | bytes 786440 | tf_op jit(solution)/shard_map/ppermute | solution.py:18
  23.9 16.2 %collective-permute-start.5 = (bf16[256,512]{0,1:T(8,128)(2,1)}, bf16[256,512]{0,1:T(8,128)(2,1)}, u32[]{:S(2)}, u32[]{:S(2)}) collective-permute-start(bf16[256,512]{0,1:T(8,128)(2,1)} %collective-permute-done.4), channel_id=1, source_target_pairs={{0,1},{1,2},{2,3},{3,4},{4,5},{5,6},{6,7},{7,8},{8,9},{9,10},{10,1... | collective-permute-start | bytes 786440 | tf_op jit(solution)/shard_map/ppermute | solution.py:18
  26.6 4.4 %copy-start.8 = (bf16[256,512]{1,0:T(8,128)(2,1)}, bf16[256,512]{1,0:T(8,128)(2,1)S(1)}, u32[]{:S(2)}) copy-start(bf16[256,512]{1,0:T(8,128)(2,1)S(1)} %collective-permute-done.1) | copy-start | bytes 786436
  26.6 11.7 %collective-permute-start.2 = (bf16[256,512]{1,0:T(8,128)(2,1)S(1)}, bf16[256,512]{1,0:T(8,128)(2,1)}, u32[]{:S(2)}, u32[]{:S(2)}) collective-permute-start(bf16[256,512]{1,0:T(8,128)(2,1)S(1)} %collective-permute-done.1), channel_id=1, source_target_pairs={{0,1},{1,2},{2,3},{3,4},{4,5},{5,6},{6,7},{7,8},{8,9},{9,10},{10,1... | collective-permute-start | bytes 786440 | tf_op jit(solution)/shard_map/ppermute | solution.py:18
  53.6 1.6 copy-start.3
  53.6 1.9 %copy-start.9 = (f32[1024]{0:T(1024)S(1)}, f32[1024]{0:T(1024)}, u32[]{:S(2)}) copy-start(f32[1024]{0:T(1024)} %param.14) | copy-start | bytes 12292
  55.3 1.1 copy-start.1
  56.4 51.6 %copy-start.11 = (bf16[1,1024,512]{2,1,0:T(8,128)(2,1)S(1)}, bf16[1,1024,512]{2,1,0:T(8,128)(2,1)}, u32[]{:S(2)}) copy-start(bf16[1,1024,512]{2,1,0:T(8,128)(2,1)} %param.15) | copy-start | bytes 3145732
  116.2 4.1 %copy-start.10 = (f32[256,2]{0,1:T(2,128)S(1)}, f32[256,2]{0,1:T(2,128)}, u32[]{:S(2)}) copy-start(f32[256,2]{0,1:T(2,128)} %param.19) | copy-start | bytes 6148
  116.2 52.7 %all-to-all-start.1 = ((bf16[8,128,1024]{2,1,0:T(8,128)(2,1)}), bf16[8,128,1024]{2,1,0:T(8,128)(2,1)S(1)}, u32[]{:S(2)}, u32[]{:S(2)}) async-start(bf16[8,128,1024]{2,1,0:T(8,128)(2,1)} %bitcast.53), calls=%async_computation.1 | async-start | bytes 4194304 | tf_op jit(solution)/shard_map/all_to_all | solution.py:81
  174.1 2.7 %copy-start.2 = (f32[256,1024]{1,0:T(8,128)S(1)}, f32[256,1024]{1,0:T(8,128)}, u32[]{:S(2)}) copy-start(f32[256,1024]{1,0:T(8,128)} %copy-done.1) | copy-start | bytes 3145732
  174.1 2.7 %copy-start.4 = (bf16[256,1024]{1,0:T(8,128)(2,1)S(1)}, bf16[256,1024]{1,0:T(8,128)(2,1)}, u32[]{:S(2)}) copy-start(bf16[256,1024]{1,0:T(8,128)(2,1)} %param.13) | copy-start | bytes 1572868
where the time goes:
time: 178 us
  waiting for transfers between devices  67.1 us (38%)
  blocking collectives  51.6 us (29%)
  matrix products  21.4 us (12%)
  starting transfers between devices  17.1 us (10%)
  local copies, waits for them, and re-layouts  11.6 us (7%)
  other arithmetic  8.8 us (5%)
    all_to_all x1, blocking collectives, local(): lax.all_to_all(outgoing, 'inner', split_axis=0, concat_axis=0, tiled=True)  51.6 us
    all_to_all x1, waiting for transfers between devices, local(): lax.all_to_all(results, 'inner', split_axis=0, concat_axis=0, tiled=True)  48.5 us
    ppermute x6, waiting for transfers between devices, shifted(): lax.ppermute(value, axis, [(source, source + steps) for source in range(f...  18.6 us
    ppermute x6, starting transfers between devices, shifted(): lax.ppermute(value, axis, [(source, source + steps) for source in range(f...  13.1 us
    sub x1, matrix products, local(): expd = jnp.exp(scores - highest)  7.12 us
    dot_general x1, matrix products, feed_forward(): jnp.dot(inner_act, down_matrix, preferred_element_type=jnp.float32)  5.63 us
    dot_general x1, matrix products, local(): jnp.einsum('kgts,skd->tkgd', weights, value_heads, preferred_element_type...  5.18 us
    all_to_all x1, starting transfers between devices, local(): lax.all_to_all(results, 'inner', split_axis=0, concat_axis=0, tiled=True)  3.91 us
  transfers between devices with their start and end apart: 7, of which 6 were waited for; matrix products, arithmetic and copies ran while one was open for 4% of the time, Pallas kernels for 0%

commit v1 on v0

--- a/solution.py
+++ b/solution.py
@@ -1,8 +1,11 @@
+import functools
 import math
 
 import jax
 import jax.numpy as jnp
 from jax import lax
+from jax.experimental import pallas as pl
+from jax.experimental.pallas import tpu as pltpu
 from jax.sharding import PartitionSpec as P
 
 D = 1024
@@ -18,11 +21,268 @@
     return lax.ppermute(value, axis, [(source, source + steps) for source in range(first, last)])
 
 
-def feed_forward(rows, gate_matrix, up_matrix, down_matrix):
-    gate_part = jnp.dot(rows, gate_matrix, preferred_element_type=jnp.float32)
-    up_part = jnp.dot(rows, up_matrix, preferred_element_type=jnp.float32)
-    inner_act = (jax.nn.silu(gate_part) * up_part).astype(jnp.bfloat16)
-    return jnp.dot(inner_act, down_matrix, preferred_element_type=jnp.float32).astype(jnp.bfloat16)
+MESH = pl.DeviceIdType.MESH
+CHUNKS = 4
+
+
+def expert_kernel(
+    lanes, normed_ref, stream_ref, shares_ref, gate_ref, up_ref, down_ref, out_ref,
+    rows, parts, mate_in, line_in, share_in,
+    share_send, share_recv, row_send, row_recv, mate_send, mate_recv,
+    give_send, give_recv, sum_send, sum_recv,
+):
+    inner = lax.axis_index("inner")
+    spots = lanes // 2
+    spot, core = inner // 2, inner % 2
+    mate = 2 * spot + (1 - core)
+    tok_rows = normed_ref.shape[0]
+    piece = tok_rows // CHUNKS
+
+    def at_piece(k):
+        return pl.ds(k * piece, piece)
+
+    def remote(src, dst, send, recv, to):
+        return pltpu.make_async_remote_copy(
+            src_ref=src, dst_ref=dst, send_sem=send, recv_sem=recv,
+            device_id={"inner": to}, device_id_type=MESH,
+        )
+
+    above, below = inner + 2, inner - 2
+    has_above, has_below = spot < spots - 1, spot > 0
+
+    barrier = pltpu.get_barrier_semaphore()
+
+    @pl.loop(1, lanes)
+    def _(step):
+        pl.semaphore_signal(
+            barrier, inc=1, device_id={"inner": lax.rem(inner + step, lanes)}, device_id_type=MESH
+        )
+
+    pl.semaphore_wait(barrier, lanes - 1)
+
+    def row_copy(src, where, sem, k, to):
+        return remote(src, rows.at[where, core, at_piece(k)], row_send.at[sem, k], row_recv.at[where, k], to)
+
+    def mate_copy(src, where, k):
+        return remote(src, rows.at[where, core, at_piece(k)], mate_send.at[where, k], mate_recv.at[where, k], mate)
+
+    def give_copy(where):
+        return remote(parts.at[where, 1 - core], mate_in.at[where], give_send.at[where], give_recv.at[where], mate)
+
+    def sum_copy(where, slot, k, to):
+        return remote(
+            parts.at[where, core, at_piece(k)], line_in.at[slot, at_piece(k)],
+            sum_send.at[where, k], sum_recv.at[slot, k], to,
+        )
+
+    for k in range(CHUNKS):
+        own = normed_ref.at[at_piece(k)]
+
+        @pl.when(has_above)
+        def _():
+            row_copy(own, spot, spot, k, above).start()
+
+        @pl.when(has_below)
+        def _():
+            row_copy(own, spot, spots, k, below).start()
+
+        mate_copy(own, spot, k).start()
+
+    def share_copy(to):
+        return remote(shares_ref.at[to], share_in.at[inner], share_send.at[to], share_recv.at[inner], to)
+
+    @pl.loop(1, lanes)
+    def _(step):
+        share_copy(lax.rem(inner + step, lanes)).start()
+
+    share_in[inner] = shares_ref[inner]
+    rows[spot, core] = normed_ref[...]
+
+    @pl.loop(1, lanes)
+    def _(step):
+        source = lax.rem(inner + step, lanes)
+        remote(
+            shares_ref.at[source], share_in.at[source], share_send.at[source], share_recv.at[source], source
+        ).wait_recv()
+
+    def experts_on(where):
+        @pl.loop(0, 2)
+        def _(side):
+            block = rows[where, side]
+            gate_part = jnp.dot(block, gate_ref[0], preferred_element_type=jnp.float32)
+            up_part = jnp.dot(block, up_ref[0], preferred_element_type=jnp.float32)
+            act = (gate_part / (1.0 + jnp.exp(-gate_part)) * up_part).astype(jnp.bfloat16)
+            result = jnp.dot(act, down_ref[0], preferred_element_type=jnp.float32)
+            share = share_in[2 * where + side]
+            row_id = lax.broadcasted_iota(jnp.int32, (tok_rows, tok_rows), 0)
+            col_id = lax.broadcasted_iota(jnp.int32, (tok_rows, tok_rows), 1)
+            column = jnp.sum(
+                jnp.where(row_id == col_id, jnp.broadcast_to(share, (tok_rows, tok_rows)), 0.0),
+                axis=1, keepdims=True,
+            )
+            result = result.astype(jnp.bfloat16).astype(jnp.float32)
+            parts[where, side] = (result * column).astype(jnp.bfloat16)
+
+        give_copy(where).start()
+
+    def take_rows(where, onward, to):
+        for k in range(CHUNKS):
+            here = rows.at[where, core, at_piece(k)]
+            row_copy(here, where, where, k, to).wait_recv()
+
+            @pl.when(onward)
+            def _():
+                row_copy(here, where, where, k, to).start()
+
+            mate_copy(here, where, k).start()
+        for k in range(CHUNKS):
+            mate_copy(rows.at[where, core, at_piece(k)], where, k).wait_recv()
+
+    def pass_sum(where, slot_to, more, to):
+        give_copy(where).wait_recv()
+        for k in range(CHUNKS):
+            at = at_piece(k)
+
+            @pl.when(more)
+            def _():
+                sum_copy(where, where, k, to).wait_recv()
+                parts[where, core, at] = (
+                    parts[where, core, at].astype(jnp.float32)
+                    + mate_in[where, at].astype(jnp.float32)
+                    + line_in[where, at].astype(jnp.float32)
+                ).astype(jnp.bfloat16)
+
+            @pl.when(jnp.logical_not(more))
+            def _():
+                parts[where, core, at] = (
+                    parts[where, core, at].astype(jnp.float32) + mate_in[where, at].astype(jnp.float32)
+                ).astype(jnp.bfloat16)
+
+            sum_copy(where, slot_to, k, to).start()
+
+    for k in range(CHUNKS):
+        mate_copy(normed_ref.at[at_piece(k)], spot, k).wait_recv()
+    experts_on(spot)
+
+    @pl.loop(1, max(2 * spots - 2, 1))
+    def _(time):
+        low, high = spot - time, spot + time
+
+        @pl.when(low >= 0)
+        def _():
+            take_rows(low, has_above, jnp.minimum(above, lanes - 2 + core))
+
+        @pl.when(high < spots)
+        def _():
+            take_rows(high, has_below, jnp.maximum(below, core))
+
+        @pl.when(low >= 0)
+        def _():
+            experts_on(low)
+
+        @pl.when(high < spots)
+        def _():
+            experts_on(high)
+
+        down = 2 * spots - 2 - spot - time
+
+        @pl.when((down >= 0) & (down < spot))
+        def _():
+            pass_sum(down, jnp.where(down == spot - 1, down, down), has_above, below)
+
+        up = time - spot
+
+        @pl.when((up > spot) & (up < spots))
+        def _():
+            pass_sum(up, jnp.where(up == spot + 1, spots, up), has_below, above)
+
+    give_copy(spot).wait_recv()
+    for k in range(CHUNKS):
+        at = at_piece(k)
+        out = parts[spot, core, at].astype(jnp.float32) + mate_in[spot, at].astype(jnp.float32)
+        stash = stream_ref[at, :] + out
+        out_ref[at, :] = stash.astype(jnp.bfloat16)
+
+        @pl.when(has_above & has_below)
+        def _():
+            sum_copy(spot, spot, k, above).wait_recv()
+            sum_copy(spot, spots, k, above).wait_recv()
+            out_ref[at, :] = (
+                stash + line_in[spot, at].astype(jnp.float32) + line_in[spots, at].astype(jnp.float32)
+            ).astype(jnp.bfloat16)
+
+        @pl.when(has_above & jnp.logical_not(has_below))
+        def _():
+            sum_copy(spot, spot, k, above).wait_recv()
+            out_ref[at, :] = (stash + line_in[spot, at].astype(jnp.float32)).astype(jnp.bfloat16)
+
+        @pl.when(has_below & jnp.logical_not(has_above))
+        def _():
+            sum_copy(spot, spots, k, below).wait_recv()
+            out_ref[at, :] = (stash + line_in[spots, at].astype(jnp.float32)).astype(jnp.bfloat16)
+
+    @pl.loop(1, lanes)
+    def _(step):
+        share_copy(lax.rem(inner + step, lanes)).wait_send()
+
+    for k in range(CHUNKS):
+        own = normed_ref.at[at_piece(k)]
+
+        @pl.when(has_above)
+        def _():
+            row_copy(own, spot, spot, k, above).wait_send()
+
+        @pl.when(has_below)
+        def _():
+            row_copy(own, spot, spots, k, below).wait_send()
+
+        mate_copy(own, spot, k).wait_send()
+
+    @pl.loop(0, spots)
+    def _(where):
+        give_copy(where).wait_send()
+
+        @pl.when(where != spot)
+        def _():
+            to = jnp.where(where < spot, jnp.minimum(above, lanes - 2 + core), jnp.maximum(below, core))
+            back = jnp.where(where < spot, inner - 2, inner + 2)
+            onward = ((where < spot) & has_above) | ((where > spot) & has_below)
+            for k in range(CHUNKS):
+                here = rows.at[where, core, at_piece(k)]
+                mate_copy(here, where, k).wait_send()
+                sum_copy(where, where, k, back).wait_send()
+
+                @pl.when(onward)
+                def _():
+                    row_copy(here, where, where, k, to).wait_send()
+
+
+def expert_layer(lanes, normed, stream, shares, w_gate, w_up, w_down):
+    tok_rows, width = normed.shape
+    spots = lanes // 2
+    vmem = pl.BlockSpec(memory_space=pltpu.VMEM)
+    dma = pltpu.SemaphoreType.DMA
+    return pl.pallas_call(
+        functools.partial(expert_kernel, lanes),
+        out_shape=jax.ShapeDtypeStruct((tok_rows, width), jnp.bfloat16),
+        in_specs=[vmem] * 6,
+        out_specs=vmem,
+        scratch_shapes=[
+            pltpu.VMEM((spots, 2, tok_rows, width), jnp.bfloat16),
+            pltpu.VMEM((spots, 2, tok_rows, width), jnp.bfloat16),
+            pltpu.VMEM((spots, tok_rows, width), jnp.bfloat16),
+            pltpu.VMEM((spots + 1, tok_rows, width), jnp.bfloat16),
+            pltpu.VMEM((lanes, 1, tok_rows), jnp.float32),
+            dma((lanes,)), dma((lanes,)),
+            dma((spots + 1, CHUNKS)), dma((spots, CHUNKS)),
+            dma((spots, CHUNKS)), dma((spots, CHUNKS)),
+            dma((spots,)), dma((spots,)),
+            dma((spots, CHUNKS)), dma((spots + 1, CHUNKS)),
+        ],
+        compiler_params=pltpu.CompilerParams(
+            collective_id=0, has_side_effects=True, vmem_limit_bytes=60 * 1024 * 1024
+        ),
+    )(normed, stream, shares, w_gate, w_up, w_down)
 
 
 def local(queries, keys, values, residual, norm_gain, w_gate, w_up, w_down, routes, gates):
@@ -56,36 +316,9 @@
     mean_sq = jnp.mean(stream * stream, -1, keepdims=True)
     normed = (stream * lax.rsqrt(mean_sq + 1e-06) * norm_gain).astype(jnp.bfloat16)
     owners = lax.axis_size("inner")
-    capacity = 4 * tok_rows // owners
-    picks = routes.reshape(-1)
-    one_hot = (picks[:, None] == jnp.arange(owners, dtype=jnp.int32)[None, :]).astype(jnp.int32)
-    order_rank = jnp.sum((jnp.cumsum(one_hot, 0) - 1) * one_hot, 1)
-    slot_index = picks * capacity + order_rank
-    slot_pair = slot_index.reshape(tok_rows, 2)
-    slot_grid = jnp.arange(owners * capacity, dtype=jnp.int32)[:, None]
-    placing = ((slot_pair[None, :, 0] == slot_grid) | (slot_pair[None, :, 1] == slot_grid)).astype(
-        jnp.bfloat16
-    )
-    outgoing = (
-        jnp.dot(placing, normed, preferred_element_type=jnp.float32)
-        .astype(jnp.bfloat16)
-        .reshape(owners, capacity, D)
-    )
-    gate_matrix = w_gate[0]
-    up_matrix = w_up[0]
-    down_matrix = w_down[0]
-    arrived = lax.all_to_all(outgoing, "inner", split_axis=0, concat_axis=0, tiled=True)
-    results = feed_forward(arrived.reshape(-1, D), gate_matrix, up_matrix, down_matrix).reshape(
-        arrived.shape
-    )
-    returned = lax.all_to_all(results, "inner", split_axis=0, concat_axis=0, tiled=True)
-    picked = (
-        returned.reshape(owners * capacity, D)[slot_index]
-        .astype(jnp.float32)
-        .reshape(tok_rows, 2, D)
-    )
-    mixture = jnp.sum(gates[:, :, None] * picked, 1)
-    return (stream + mixture).astype(jnp.bfloat16)
+    named = routes.T[:, None, :] == jnp.arange(owners, dtype=jnp.int32)[None, :, None]
+    shares = jnp.sum(jnp.where(named, gates.T[:, None, :], 0.0), 0)[:, None, :]
+    return expert_layer(owners, normed, stream, shares, w_gate, w_up, w_down)
 
 
 def solution(mesh):

time: 178 us -> 134 us (0.75)
  Pallas kernels: 0 us -> 79.7 us
  blocking collectives: 51.6 us -> 0 us
  waiting for transfers between devices: 67.1 us -> 19.3 us
  matrix products: 21.4 us -> 10.1 us
  local copies, waits for them, and re-layouts: 11.6 us -> 5.87 us
  starting transfers between devices: 17.1 us -> 13.1 us
  other arithmetic: 8.8 us -> 5.6 us
    pallas_call x0 -> x1, Pallas kernels: none -> 79.7 us  [expert_layer(): pl.pallas_call(functools.partial(expert_kernel, lanes), out_shape=jax.Sha...]
    all_to_all x1 -> x0, blocking collectives: 51.6 us -> none  [local(): lax.all_to_all(outgoing, 'inner', split_axis=0, concat_axis=0, tiled=True)]
    all_to_all x1 -> x0, waiting for transfers between devices: 48.5 us -> none  [local(): lax.all_to_all(results, 'inner', split_axis=0, concat_axis=0, tiled=True)]
    dot_general x3 -> x0, matrix products: 9.06 us -> none  [the longest x1 5.63 us: feed_forward(): jnp.dot(inner_act, down_matrix, preferred_element_type=jnp.float32)]
    all_to_all x1 -> x0, starting transfers between devices: 3.91 us -> none  [local(): lax.all_to_all(results, 'inner', split_axis=0, concat_axis=0, tiled=True)]
    gather x1 -> x0, local copies, waits for them, and re-layouts: 2.78 us -> none  [local(): returned.reshape(owners * capacity, D)[slot_index].astype(jnp.float32)]
    convert_element_type x1 -> x0, local copies, waits for them, and re-layouts: 2.37 us -> none  [local(): picked = returned.reshape(owners * capacity, D)[slot_index].astype(jnp.fl...]
    reduce_sum x2 -> x1, other arithmetic: 2.73 us -> 0.71 us  [local(): shares = jnp.sum(jnp.where(named, gates.T[:, None, :], 0.0), 0)[:, None, :]]
  transfers between devices with their start and end apart: 7 -> 6, of which waited for: 6 -> 5; matrix products, arithmetic and copies ran while one was open for 4% -> 4% of each run, Pallas kernels for 0% -> 0%
where the time goes in v1:
time: 134 us
  Pallas kernels  79.7 us (59%)
  waiting for transfers between devices  19.3 us (14%)
  starting transfers between devices  13.1 us (10%)
  matrix products  10.1 us (8%)
  local copies, waits for them, and re-layouts  5.87 us (4%)
  other arithmetic  5.6 us (4%)
    pallas_call x1, Pallas kernels, expert_layer(): pl.pallas_call(functools.partial(expert_kernel, lanes), out_shape=jax.Sha...  79.7 us
    ppermute x6, waiting for transfers between devices, shifted(): lax.ppermute(value, axis, [(source, source + steps) for source in range(f...  19.3 us
    ppermute x6, starting transfers between devices, shifted(): lax.ppermute(value, axis, [(source, source + steps) for source in range(f...  13.1 us
    sub x1, matrix products, local(): expd = jnp.exp(scores - highest)  6.01 us
    dot_general x1, matrix products, local(): jnp.einsum('kgts,skd->tkgd', weights, value_heads, preferred_element_type...  4.1 us
    unnamed x6, local copies, waits for them, and re-layouts  3 us
  transfers between devices with their start and end apart: 6, of which 5 were waited for; matrix products, arithmetic and copies ran while one was open for 4% of the time, Pallas kernels for 0%

profile of v1, /device:TPU:4, one launch (start us, length us, event | category | flops | bytes accessed | tf_op | source)
XLA Modules:
  0.0 133.9 jit_solution(518792690462585599)
XLA Ops:
  0.0 1.9 %collective-permute-start = (bf16[256,512]{1,0:T(8,128)(2,1)}, bf16[256,512]{1,0:T(8,128)(2,1)S(1)}, u32[]{:S(2)}, u32[]{:S(2)}) collective-permute-start(bf16[256,512]{1,0:T(8,128)(2,1)} %param.12), channel_id=1, source_target_pairs={{0,1},{1,2},{2,3},{3,4},{4,5},{5,6},{6,7},{7,8},{8,9},{9,10},{10,1... | collective-permute-start | bytes 786440 | tf_op jit(solution)/shard_map/ppermute | solution.py:21
  1.9 1.1 copy.23
  3.0 3.6 %collective-permute-start.3 = (bf16[256,512]{0,1:T(8,128)(2,1)S(1)}, bf16[256,512]{0,1:T(8,128)(2,1)S(1)}, u32[]{:S(2)}, u32[]{:S(2)}) collective-permute-start(bf16[256,512]{0,1:T(8,128)(2,1)S(1)} %copy.23), channel_id=1, source_target_pairs={{0,1},{1,2},{2,3},{3,4},{4,5},{5,6},{6,7},{7,8},{8,9},{9,10},{10,1... | collective-permute-start | bytes 786440 | tf_op jit(solution)/shard_map/ppermute | solution.py:21
  6.6 4.9 %collective-permute-done = bf16[256,512]{1,0:T(8,128)(2,1)S(1)} collective-permute-done((bf16[256,512]{1,0:T(8,128)(2,1)}, bf16[256,512]{1,0:T(8,128)(2,1)S(1)}, u32[]{:S(2)}, u32[]{:S(2)}) %collective-permute-start) | collective-permute-done | bytes 262176 | tf_op jit(solution)/shard_map/ppermute | solution.py:21
  11.5 1.9 %collective-permute-start.1 = (bf16[256,512]{1,0:T(8,128)(2,1)S(1)}, bf16[256,512]{1,0:T(8,128)(2,1)S(1)}, u32[]{:S(2)}, u32[]{:S(2)}) collective-permute-start(bf16[256,512]{1,0:T(8,128)(2,1)S(1)} %collective-permute-done), channel_id=1, source_target_pairs={{0,1},{1,2},{2,3},{3,4},{4,5},{5,6},{6,7},{7,8},{8,9},{9,10},{10,1... | collective-permute-start | bytes 786440 | tf_op jit(solution)/shard_map/ppermute | solution.py:21
  13.4 0.9 collective-permute-done.3
  14.3 1.9 %collective-permute-start.4 = (bf16[256,512]{0,1:T(8,128)(2,1)S(1)}, bf16[256,512]{0,1:T(8,128)(2,1)}, u32[]{:S(2)}, u32[]{:S(2)}) collective-permute-start(bf16[256,512]{0,1:T(8,128)(2,1)S(1)} %collective-permute-done.3), channel_id=1, source_target_pairs={{0,1},{1,2},{2,3},{3,4},{4,5},{5,6},{6,7},{7,8},{8,9},{9,10},{10,1... | collective-permute-start | bytes 786440 | tf_op jit(solution)/shard_map/ppermute | solution.py:21
  16.2 0.7 select_reduce_fusion
  16.9 5.8 %collective-permute-done.1 = bf16[256,512]{1,0:T(8,128)(2,1)S(1)} collective-permute-done((bf16[256,512]{1,0:T(8,128)(2,1)S(1)}, bf16[256,512]{1,0:T(8,128)(2,1)S(1)}, u32[]{:S(2)}, u32[]{:S(2)}) %collective-permute-start.1) | collective-permute-done | bytes 262176 | tf_op jit(solution)/shard_map/ppermute | solution.py:21
  22.8 1.9 %collective-permute-start.2 = (bf16[256,512]{1,0:T(8,128)(2,1)S(1)}, bf16[256,512]{1,0:T(8,128)(2,1)S(1)}, u32[]{:S(2)}, u32[]{:S(2)}) collective-permute-start(bf16[256,512]{1,0:T(8,128)(2,1)S(1)} %collective-permute-done.1), channel_id=1, source_target_pairs={{0,1},{1,2},{2,3},{3,4},{4,5},{5,6},{6,7},{7,8},{8,9},{9,10},{10,1... | collective-permute-start | bytes 786440 | tf_op jit(solution)/shard_map/ppermute | solution.py:21
  24.7 1.4 %reshape.39 = bf16[256,4,2,128]{3,2,1,0:T(2,128)(2,1)S(1)} reshape(bf16[256,1024]{1,0:T(8,128)(2,1)} %param.10) | data formatting | bytes 1048576 | tf_op jit(solution)/shard_map/reshape | solution.py:300
  26.1 0.6 broadcast_in_dim.37.shares_ref
  26.7 1.9 %collective-permute-start.5 = (bf16[256,512]{0,1:T(8,128)(2,1)}, bf16[256,512]{0,1:T(8,128)(2,1)}, u32[]{:S(2)}, u32[]{:S(2)}) collective-permute-start(bf16[256,512]{0,1:T(8,128)(2,1)} %collective-permute-done.4), channel_id=1, source_target_pairs={{0,1},{1,2},{2,3},{3,4},{4,5},{5,6},{6,7},{7,8},{8,9},{9,10},{10,1... | collective-permute-start | bytes 786440 | tf_op jit(solution)/shard_map/ppermute | solution.py:21
  29.0 5.1 %collective-permute-done.2 = bf16[256,512]{1,0:T(8,128)(2,1)S(1)} collective-permute-done((bf16[256,512]{1,0:T(8,128)(2,1)S(1)}, bf16[256,512]{1,0:T(8,128)(2,1)S(1)}, u32[]{:S(2)}, u32[]{:S(2)}) %collective-permute-start.2) | collective-permute-done | bytes 262176 | tf_op jit(solution)/shard_map/ppermute | solution.py:21
  34.0 1.0 pad_maximum_fusion
  35.1 0.5 copy.22
  35.6 2.7 %collective-permute-done.5 = bf16[256,512]{0,1:T(8,128)(2,1)} collective-permute-done((bf16[256,512]{0,1:T(8,128)(2,1)}, bf16[256,512]{0,1:T(8,128)(2,1)}, u32[]{:S(2)}, u32[]{:S(2)}) %collective-permute-start.5) | collective-permute-done | bytes 262176 | tf_op jit(solution)/shard_map/ppermute | solution.py:21
  38.3 1.2 pad_maximum_fusion.1
  39.5 6.0 %fusion.19 = (f32[4,2,256]{2,1,0:T(2,128)S(1)}, f32[4,2,256,1024]{2,3,1,0:T(8,128)}) fusion(pred[256,1024]{0,1:T(8,128)(4,1)S(1)} %compare_and_fusion, bf16[1024,4,128,1]{0,2,3,1:T(8,128)(2,1)S(1)} %bitcast.30, bf16[256,4,2,128]{3,2,1,0:T(2,128)(2,1)S(1)} %reshape.39), kind=kOutput, calls=%fused_computation.29 | convolution fusion | flops 545260544 | bytes 10231808 | tf_op jit(solution)/shard_map/sub | solution.py:311
  45.5 4.1 %fusion.7 = f32[4,128,2,256]{3,1,2,0:T(8,128)S(1)} fusion(bf16[1024,4,128,1]{0,2,3,1:T(8,128)(2,1)S(1)} %bitcast.29, f32[4,2,256,1024]{2,3,1,0:T(8,128)} %get-tuple-element.8, f32[4,2,256]{2,1,0:T(2,128)S(1)} %get-tuple-element.7), kind=kOutput, calls=%fused_computation.10 | convolution fusion | flops 541589504 | bytes 10493952 | tf_op jit(solution)/shard_map/kgts,skd->tkgd/dot_general | solution.py:313
  49.9 1.3 multiply_reduce_fusion
  51.2 1.1 multiply_convert_fusion.normed_ref
  52.4 79.7 %shard_map.100 = bf16[256,1024]{1,0:T(8,128)(2,1)} custom-call(bf16[256,1024]{1,0:T(8,128)(2,1)} %multiply_convert_fusion.normed_ref, f32[256,1024]{1,0:T(8,128)} %copy-done, f32[8,1,256]{2,1,0:T(1,128)} %broadcast_in_dim.37.shares_ref, bf16[1,1024,512]{2,1,0:T(8,128)(2,1)} %gate_ref.1, bf16[1,1024,512]{2,1,0:T(8,128)(2,1)} %up_ref.1, ...), custom_call_target="tpu_custom_call" | custom-call | tf_op jit(solution)/shard_map/pallas_call | solution.py:265
  132.0 1.9 %copy.48 = bf16[256,1024]{1,0:T(8,128)(2,1)} copy(bf16[256,1024]{1,0:T(8,128)(2,1)} %shard_map.100) | data formatting | bytes 1048576
  (11 shorter events, 0.7 us)
Async XLA Ops:
  0.0 11.5 %collective-permute-start = (bf16[256,512]{1,0:T(8,128)(2,1)}, bf16[256,512]{1,0:T(8,128)(2,1)S(1)}, u32[]{:S(2)}, u32[]{:S(2)}) collective-permute-start(bf16[256,512]{1,0:T(8,128)(2,1)} %param.12), channel_id=1, source_target_pairs={{0,1},{1,2},{2,3},{3,4},{4,5},{5,6},{6,7},{7,8},{8,9},{9,10},{10,1... | collective-permute-start | bytes 786440 | tf_op jit(solution)/shard_map/ppermute | solution.py:21
  3.0 11.3 %collective-permute-start.3 = (bf16[256,512]{0,1:T(8,128)(2,1)S(1)}, bf16[256,512]{0,1:T(8,128)(2,1)S(1)}, u32[]{:S(2)}, u32[]{:S(2)}) collective-permute-start(bf16[256,512]{0,1:T(8,128)(2,1)S(1)} %copy.23), channel_id=1, source_target_pairs={{0,1},{1,2},{2,3},{3,4},{4,5},{5,6},{6,7},{7,8},{8,9},{9,10},{10,1... | collective-permute-start | bytes 786440 | tf_op jit(solution)/shard_map/ppermute | solution.py:21
  11.5 11.3 %collective-permute-start.1 = (bf16[256,512]{1,0:T(8,128)(2,1)S(1)}, bf16[256,512]{1,0:T(8,128)(2,1)S(1)}, u32[]{:S(2)}, u32[]{:S(2)}) collective-permute-start(bf16[256,512]{1,0:T(8,128)(2,1)S(1)} %collective-permute-done), channel_id=1, source_target_pairs={{0,1},{1,2},{2,3},{3,4},{4,5},{5,6},{6,7},{7,8},{8,9},{9,10},{10,1... | collective-permute-start | bytes 786440 | tf_op jit(solution)/shard_map/ppermute | solution.py:21
  14.3 12.4 %collective-permute-start.4 = (bf16[256,512]{0,1:T(8,128)(2,1)S(1)}, bf16[256,512]{0,1:T(8,128)(2,1)}, u32[]{:S(2)}, u32[]{:S(2)}) collective-permute-start(bf16[256,512]{0,1:T(8,128)(2,1)S(1)} %collective-permute-done.3), channel_id=1, source_target_pairs={{0,1},{1,2},{2,3},{3,4},{4,5},{5,6},{6,7},{7,8},{8,9},{9,10},{10,1... | collective-permute-start | bytes 786440 | tf_op jit(solution)/shard_map/ppermute | solution.py:21
  22.8 11.3 %collective-permute-start.2 = (bf16[256,512]{1,0:T(8,128)(2,1)S(1)}, bf16[256,512]{1,0:T(8,128)(2,1)S(1)}, u32[]{:S(2)}, u32[]{:S(2)}) collective-permute-start(bf16[256,512]{1,0:T(8,128)(2,1)S(1)} %collective-permute-done.1), channel_id=1, source_target_pairs={{0,1},{1,2},{2,3},{3,4},{4,5},{5,6},{6,7},{7,8},{8,9},{9,10},{10,1... | collective-permute-start | bytes 786440 | tf_op jit(solution)/shard_map/ppermute | solution.py:21
  26.7 11.6 %collective-permute-start.5 = (bf16[256,512]{0,1:T(8,128)(2,1)}, bf16[256,512]{0,1:T(8,128)(2,1)}, u32[]{:S(2)}, u32[]{:S(2)}) collective-permute-start(bf16[256,512]{0,1:T(8,128)(2,1)} %collective-permute-done.4), channel_id=1, source_target_pairs={{0,1},{1,2},{2,3},{3,4},{4,5},{5,6},{6,7},{7,8},{8,9},{9,10},{10,1... | collective-permute-start | bytes 786440 | tf_op jit(solution)/shard_map/ppermute | solution.py:21
  49.6 1.6 %copy-start.1 = (f32[1024]{0:T(1024)S(1)}, f32[1024]{0:T(1024)}, u32[]{:S(2)}) copy-start(f32[1024]{0:T(1024)} %param.14) | copy-start | bytes 12292
  51.2 1.2 copy-start

commit v2 on v1

--- a/solution.py
+++ b/solution.py
@@ -15,19 +15,14 @@
 BACK = 3
 
 
-def shifted(value, axis, steps):
-    count = lax.axis_size(axis)
-    first, last = (max(0, -steps), min(count, count - steps))
-    return lax.ppermute(value, axis, [(source, source + steps) for source in range(first, last)])
-
-
 MESH = pl.DeviceIdType.MESH
 CHUNKS = 4
 
 
 def expert_kernel(
-    lanes, normed_ref, stream_ref, shares_ref, gate_ref, up_ref, down_ref, out_ref,
-    rows, parts, mate_in, line_in, share_in,
+    lanes, total, query_ref, key_ref, value_ref, residual_ref, gain_ref, route_ref, pick_ref,
+    gate_ref, up_ref, down_ref, out_ref,
+    key_halo, value_halo, top, mass, stream, shares_ref, halo_send, halo_recv, rows, parts, mate_in, line_in, share_in,
     share_send, share_recv, row_send, row_recv, mate_send, mate_recv,
     give_send, give_recv, sum_send, sum_recv,
 ):
@@ -35,7 +30,9 @@
     spots = lanes // 2
     spot, core = inner // 2, inner % 2
     mate = 2 * spot + (1 - core)
-    tok_rows = normed_ref.shape[0]
+    tok_rows = query_ref.shape[0]
+    groups = QH // KVH
+    place = lax.axis_index("outer") * lanes + inner
     piece = tok_rows // CHUNKS
 
     def at_piece(k):
@@ -58,7 +55,136 @@
             barrier, inc=1, device_id={"inner": lax.rem(inner + step, lanes)}, device_id_type=MESH
         )
 
-    pl.semaphore_wait(barrier, lanes - 1)
+    def whole_id(to):
+        return {"outer": to // lanes, "inner": lax.rem(to, lanes)}
+
+    expected = lanes - 1
+    for shift in (-2, -1, 1, 2):
+        other = place + shift
+        reaches = (other >= 0) & (other < total)
+
+        @pl.when(reaches)
+        def _():
+            pl.semaphore_signal(barrier, inc=1, device_id=whole_id(other), device_id_type=MESH)
+
+        expected = expected + reaches.astype(jnp.int32)
+
+    @pl.loop(0, lanes)
+    def _(expert):
+        chosen = jnp.where(route_ref[...] == expert, pick_ref[...], 0.0)
+        shares_ref[expert] = jnp.sum(chosen, axis=0, keepdims=True)
+
+    pl.semaphore_wait(barrier, expected)
+
+    even = core == 0
+    halos = ((key_ref, key_halo), (value_ref, value_halo))
+
+    def halo_copy(kind, held, ahead, lane):
+        own_ref, halo = halos[kind]
+        src = own_ref if held == 0 else halo.at[held - 1]
+        return pltpu.make_async_remote_copy(
+            src_ref=src, dst_ref=halo.at[held + ahead - 1],
+            send_sem=halo_send.at[kind, lane], recv_sem=halo_recv.at[kind, held + ahead - 1],
+            device_id=whole_id(jnp.minimum(place + ahead, total - 1)), device_id_type=MESH,
+        )
+
+    goes_one = place + 1 < total
+    goes_two = even & (place + 2 < total)
+    plan = (
+        (0, 1, goes_one),
+        (0, 2, goes_two),
+        (1, 1, even & (place >= 1)),
+        (1, 2, goes_two & (place >= 1)),
+        (2, 1, even & (place >= 2)),
+    )
+
+    def halo_start(kind, lane):
+        held, ahead, active = plan[lane]
+
+        @pl.when(active)
+        def _():
+            halo_copy(kind, held, ahead, lane).start()
+
+    def halo_wait(kind, held):
+        own_ref, halo = halos[kind]
+
+        @pl.when(place >= held)
+        def _():
+            pltpu.make_async_remote_copy(
+                src_ref=own_ref, dst_ref=halo.at[held - 1],
+                send_sem=halo_send.at[kind, 0], recv_sem=halo_recv.at[kind, held - 1],
+                device_id=whole_id(jnp.maximum(place - 1, 0)), device_id_type=MESH,
+            ).wait_recv()
+
+    for lane in (1, 0):
+        halo_start(0, lane)
+    for lane in (1, 0):
+        halo_start(1, lane)
+
+    def attend(held):
+        @pl.loop(0, KVH)
+        def _(head):
+            wide = pl.ds(pl.multiple_of(head * groups * DH, groups * DH), groups * DH)
+            narrow = pl.ds(pl.multiple_of(head * DH, DH), DH)
+            asked = query_ref[:, wide]
+            if held == 0:
+                keys, vals = key_ref[:, narrow], value_ref[:, narrow]
+            else:
+                keys, vals = key_halo[held - 1, :, narrow], value_halo[held - 1, :, narrow]
+            mixed = []
+            for group in range(groups):
+                scores = lax.dot_general(
+                    asked[:, group * DH : (group + 1) * DH], keys, (((1,), (1,)), ((), ())),
+                    preferred_element_type=jnp.float32,
+                ) * (1.0 / math.sqrt(DH))
+                if held == 0:
+                    row_id = lax.broadcasted_iota(jnp.int32, scores.shape, 0)
+                    col_id = lax.broadcasted_iota(jnp.int32, scores.shape, 1)
+                    scores = jnp.where(col_id <= row_id, scores, -jnp.inf)
+                highest = jnp.max(scores, -1, keepdims=True)
+                slot = head * groups + group
+                if held:
+                    highest = jnp.maximum(top[slot], highest)
+                expd = jnp.exp(scores - highest)
+                summed = jnp.sum(expd, -1, keepdims=True)
+                part = jnp.dot(expd.astype(jnp.bfloat16), vals, preferred_element_type=jnp.float32)
+                if held:
+                    keep = jnp.exp(top[slot] - highest)
+                    summed = summed + mass[slot] * keep
+                    at = pl.ds(pl.multiple_of(slot * DH, DH), DH)
+                    part = part + stream[:, at] * keep
+                top[slot] = highest
+                mass[slot] = summed
+                mixed.append(part)
+            stream[:, wide] = jnp.concatenate(mixed, 1)
+
+    attend(0)
+    for kind in range(2):
+        halo_wait(kind, 1)
+        halo_start(kind, 3)
+        halo_start(kind, 2)
+        halo_wait(kind, 2)
+        halo_start(kind, 4)
+    for held in range(1, BACK + 1):
+        if held == BACK:
+            halo_wait(0, held)
+            halo_wait(1, held)
+
+        @pl.when(place >= held)
+        def _():
+            attend(held)
+
+    @pl.loop(0, QH)
+    def _(slot):
+        at = pl.ds(pl.multiple_of(slot * DH, DH), DH)
+        attended = (stream[:, at] / mass[slot]).astype(jnp.bfloat16).astype(jnp.float32)
+        stream[:, at] = residual_ref[:, at].astype(jnp.float32) + attended
+
+    for k in range(CHUNKS):
+        at = pl.ds(k * piece, piece)
+        kept = stream[at, :]
+        mean_sq = jnp.mean(kept * kept, -1, keepdims=True)
+        rows[spot, core, at] = (kept * lax.rsqrt(mean_sq + 1e-06) * gain_ref[...]).astype(jnp.bfloat16)
 
     def row_copy(src, where, sem, k, to):
         return remote(src, rows.at[where, core, at_piece(k)], row_send.at[sem, k], row_recv.at[where, k], to)
@@ -76,7 +202,7 @@
         )
 
     for k in range(CHUNKS):
-        own = normed_ref.at[at_piece(k)]
+        own = rows.at[spot, core, at_piece(k)]
 
         @pl.when(has_above)
         def _():
@@ -96,7 +222,6 @@
         share_copy(lax.rem(inner + step, lanes)).start()
 
     share_in[inner] = shares_ref[inner]
-    rows[spot, core] = normed_ref[...]
 
     @pl.loop(1, lanes)
     def _(step):
@@ -107,7 +232,8 @@
 
     def experts_on(where):
         @pl.loop(0, 2)
-        def _(side):
+        def _(turn):
+            side = lax.rem(1 - core + turn, 2)
             block = rows[where, side]
             gate_part = jnp.dot(block, gate_ref[0], preferred_element_type=jnp.float32)
             up_part = jnp.dot(block, up_ref[0], preferred_element_type=jnp.float32)
@@ -123,7 +249,10 @@
             result = result.astype(jnp.bfloat16).astype(jnp.float32)
             parts[where, side] = (result * column).astype(jnp.bfloat16)
 
-        give_copy(where).start()
+            @pl.when(turn == 0)
+            def _():
+                give_copy(where).start()
+
 
     def take_rows(where, onward, to):
         for k in range(CHUNKS):
@@ -161,7 +290,7 @@
             sum_copy(where, slot_to, k, to).start()
 
     for k in range(CHUNKS):
-        mate_copy(normed_ref.at[at_piece(k)], spot, k).wait_recv()
+        mate_copy(rows.at[spot, core, at_piece(k)], spot, k).wait_recv()
     experts_on(spot)
 
     @pl.loop(1, max(2 * spots - 2, 1))
@@ -188,7 +317,7 @@
 
         @pl.when((down >= 0) & (down < spot))
         def _():
-            pass_sum(down, jnp.where(down == spot - 1, down, down), has_above, below)
+            pass_sum(down, down, has_above, below)
 
         up = time - spot
 
@@ -200,7 +329,7 @@
     for k in range(CHUNKS):
         at = at_piece(k)
         out = parts[spot, core, at].astype(jnp.float32) + mate_in[spot, at].astype(jnp.float32)
-        stash = stream_ref[at, :] + out
+        stash = stream[at, :] + out
         out_ref[at, :] = stash.astype(jnp.bfloat16)
 
         @pl.when(has_above & has_below)
@@ -226,7 +355,7 @@
         share_copy(lax.rem(inner + step, lanes)).wait_send()
 
     for k in range(CHUNKS):
-        own = normed_ref.at[at_piece(k)]
+        own = rows.at[spot, core, at_piece(k)]
 
         @pl.when(has_above)
         def _():
@@ -237,6 +366,13 @@
             row_copy(own, spot, spots, k, below).wait_send()
 
         mate_copy(own, spot, k).wait_send()
+
+    for kind in range(2):
+        for lane, (held, ahead, active) in enumerate(plan):
+
+            @pl.when(active)
+            def _():
+                halo_copy(kind, held, ahead, lane).wait_send()
 
     @pl.loop(0, spots)
     def _(where):
@@ -257,21 +393,29 @@
                     row_copy(here, where, where, k, to).wait_send()
 
 
-def expert_layer(lanes, normed, stream, shares, w_gate, w_up, w_down):
-    tok_rows, width = normed.shape
+def local(lanes, total, queries, keys, values, residual, norm_gain, w_gate, w_up, w_down, routes, gates):
+    tok_rows, width = queries.shape
     spots = lanes // 2
     vmem = pl.BlockSpec(memory_space=pltpu.VMEM)
     dma = pltpu.SemaphoreType.DMA
+    block = (tok_rows, width)
     return pl.pallas_call(
-        functools.partial(expert_kernel, lanes),
-        out_shape=jax.ShapeDtypeStruct((tok_rows, width), jnp.bfloat16),
-        in_specs=[vmem] * 6,
+        functools.partial(expert_kernel, lanes, total),
+        out_shape=jax.ShapeDtypeStruct(block, jnp.bfloat16),
+        in_specs=[vmem] * 10,
         out_specs=vmem,
         scratch_shapes=[
-            pltpu.VMEM((spots, 2, tok_rows, width), jnp.bfloat16),
-            pltpu.VMEM((spots, 2, tok_rows, width), jnp.bfloat16),
-            pltpu.VMEM((spots, tok_rows, width), jnp.bfloat16),
-            pltpu.VMEM((spots + 1, tok_rows, width), jnp.bfloat16),
+            pltpu.VMEM((BACK,) + keys.shape, jnp.bfloat16),
+            pltpu.VMEM((BACK,) + values.shape, jnp.bfloat16),
+            pltpu.VMEM((QH, tok_rows, 1), jnp.float32),
+            pltpu.VMEM((QH, tok_rows, 1), jnp.float32),
+            pltpu.VMEM(block, jnp.float32),
+            pltpu.VMEM((lanes, 1, tok_rows), jnp.float32),
+            dma((2, 5)), dma((2, BACK)),
+            pltpu.VMEM((spots, 2) + block, jnp.bfloat16),
+            pltpu.VMEM((spots, 2) + block, jnp.bfloat16),
+            pltpu.VMEM((spots,) + block, jnp.bfloat16),
+            pltpu.VMEM((spots + 1,) + block, jnp.bfloat16),
             pltpu.VMEM((lanes, 1, tok_rows), jnp.float32),
             dma((lanes,)), dma((lanes,)),
             dma((spots + 1, CHUNKS)), dma((spots, CHUNKS)),
@@ -282,48 +426,12 @@
         compiler_params=pltpu.CompilerParams(
             collective_id=0, has_side_effects=True, vmem_limit_bytes=60 * 1024 * 1024
         ),
-    )(normed, stream, shares, w_gate, w_up, w_down)
-
-
-def local(queries, keys, values, residual, norm_gain, w_gate, w_up, w_down, routes, gates):
-    tok_rows = queries.shape[0]
-    groups = QH // KVH
-    device_index = lax.axis_index(("outer", "inner"))
-    current = (keys, values)
-    earlier = []
-    for step_index in range(BACK):
-        current = shifted((current[0], current[1]), ("outer", "inner"), 1)
-        earlier = [current] + earlier
-    key_window = jnp.concatenate([block_pair[0] for block_pair in earlier] + [keys], 0)
-    value_window = jnp.concatenate([block_pair[1] for block_pair in earlier] + [values], 0)
-    window_rows = key_window.shape[0]
-    query_heads = queries.reshape(tok_rows, KVH, groups, DH)
-    key_heads = key_window.reshape(window_rows, KVH, DH)
-    value_heads = value_window.reshape(window_rows, KVH, DH)
-    scores = jnp.einsum(
-        "tkgd,skd->kgts", query_heads, key_heads, preferred_element_type=jnp.float32
-    ) * (1.0 / math.sqrt(DH))
-    query_pos = device_index * tok_rows + jnp.arange(tok_rows, dtype=jnp.int32)
-    key_pos = (device_index - BACK) * tok_rows + jnp.arange(window_rows, dtype=jnp.int32)
-    allowed = (key_pos[None, :] >= 0) & (key_pos[None, :] <= query_pos[:, None])
-    scores = jnp.where(allowed, scores, -jnp.inf)
-    highest = jnp.max(scores, -1, keepdims=True)
-    expd = jnp.exp(scores - highest)
-    weights = (expd / jnp.sum(expd, -1, keepdims=True)).astype(jnp.bfloat16)
-    mixed = jnp.einsum("kgts,skd->tkgd", weights, value_heads, preferred_element_type=jnp.float32)
-    attended = mixed.astype(jnp.bfloat16).reshape(tok_rows, QH * DH)
-    stream = residual.astype(jnp.float32) + attended.astype(jnp.float32)
-    mean_sq = jnp.mean(stream * stream, -1, keepdims=True)
-    normed = (stream * lax.rsqrt(mean_sq + 1e-06) * norm_gain).astype(jnp.bfloat16)
-    owners = lax.axis_size("inner")
-    named = routes.T[:, None, :] == jnp.arange(owners, dtype=jnp.int32)[None, :, None]
-    shares = jnp.sum(jnp.where(named, gates.T[:, None, :], 0.0), 0)[:, None, :]
-    return expert_layer(owners, normed, stream, shares, w_gate, w_up, w_down)
+    )(queries, keys, values, residual, norm_gain[None, :], routes.T, gates.T, w_gate, w_up, w_down)
 
 
 def solution(mesh):
     return jax.shard_map(
-        local,
+        functools.partial(local, mesh.shape["inner"], mesh.shape["outer"] * mesh.shape["inner"]),
         mesh=mesh,
         in_specs=(
             P(("outer", "inner"), None),

time: 134 us -> 109 us (0.81)
  Pallas kernels: 79.7 us -> 107 us
  waiting for transfers between devices: 19.3 us -> 0 us
  starting transfers between devices: 13.1 us -> 0 us
  matrix products: 10.1 us -> 0 us
  other arithmetic: 5.6 us -> 0 us
  local copies, waits for them, and re-layouts: 5.87 us -> 1.87 us
    pallas_call x1, Pallas kernels: 79.7 us -> 107 us  [local(): pl.pallas_call(functools.partial(expert_kernel, lanes, total), out_shape=...]
    ppermute x6 -> x0, waiting for transfers between devices: 19.3 us -> none  [shifted(): lax.ppermute(value, axis, [(source, source + steps) for source in range(f...]
    ppermute x6 -> x0, starting transfers between devices: 13.1 us -> none  [shifted(): lax.ppermute(value, axis, [(source, source + steps) for source in range(f...]
    sub x1 -> x0, matrix products: 6.01 us -> none  [local(): expd = jnp.exp(scores - highest)]
    dot_general x1 -> x0, matrix products: 4.1 us -> none  [local(): jnp.einsum('kgts,skd->tkgd', weights, value_heads, preferred_element_type...]
    concatenate x2 -> x0, other arithmetic: 2.18 us -> none  [the longest x1 1.16 us: local(): jnp.concatenate([block_pair[0] for block_pair in earlier] + [keys], 0)]
    reduce_sum x2 -> x0, other arithmetic: 1.97 us -> none  [the longest x1 1.26 us: local(): mean_sq = jnp.mean(stream * stream, -1, keepdims=True)]
    reshape x1 -> x0, local copies, waits for them, and re-layouts: 1.41 us -> none  [local(): query_heads = queries.reshape(tok_rows, KVH, groups, DH)]
  transfers between devices with their start and end apart: 6 -> 0, of which waited for: 5 -> 0; matrix products, arithmetic and copies ran while one was open for 4% -> 0% of each run, Pallas kernels for 0% -> 0%
where the time goes in v2:
time: 109 us; the launch traced here: 108 us
  Pallas kernels  107 us (98%)
  local copies, waits for them, and re-layouts  1.87 us (2%)
    pallas_call x1, Pallas kernels, local(): pl.pallas_call(functools.partial(expert_kernel, lanes, total), out_shape=...  107 us

profile of v2, /device:TPU:4, one launch (start us, length us, event | category | flops | bytes accessed | tf_op | source)
XLA Modules:
  0.0 108.4 jit_solution(6737381113261684195)
XLA Ops:
  0.0 106.5 %shard_map.100 = bf16[256,1024]{1,0:T(8,128)(2,1)} custom-call(bf16[256,1024]{1,0:T(8,128)(2,1)} %query_ref.1, bf16[256,512]{1,0:T(8,128)(2,1)} %key_ref.1, bf16[256,512]{1,0:T(8,128)(2,1)} %value_ref.1, bf16[256,1024]{1,0:T(8,128)(2,1)} %residual_ref.1, f32[1,1024]{1,0:T(1,128)} %bitcast.3, s32[2,256]{1,0:T(2,128)} %bitcast.4, f32[2,256]{1,0:T(2,128)} %bitcast.5, ...), custom_call_target="tpu_custom_call" | custom-call | tf_op jit(solution)/shard_map/pallas_call | solution.py:402
  106.5 1.9 %copy.12 = bf16[256,1024]{1,0:T(8,128)(2,1)} copy(bf16[256,1024]{1,0:T(8,128)(2,1)} %shard_map.100) | data formatting | bytes 1048576

commit v3 on v2

--- a/solution.py
+++ b/solution.py
@@ -17,6 +17,7 @@
 
 MESH = pl.DeviceIdType.MESH
 CHUNKS = 4
+HALVES = 2
 
 
 def expert_kernel(
@@ -34,9 +35,16 @@
     groups = QH // KVH
     place = lax.axis_index("outer") * lanes + inner
     piece = tok_rows // CHUNKS
+    half_rows = tok_rows // HALVES
 
     def at_piece(k):
-        return pl.ds(k * piece, piece)
+        return pl.ds(pl.multiple_of(k * piece, piece), piece)
+
+    def pieces(half):
+        return [half * (CHUNKS // HALVES) + k for k in range(CHUNKS // HALVES)]
+
+    def at_half(half):
+        return pl.ds(pl.multiple_of(half * half_rows, half_rows), half_rows)
 
     def remote(src, dst, send, recv, to):
         return pltpu.make_async_remote_copy(
@@ -192,8 +200,12 @@
     def mate_copy(src, where, k):
         return remote(src, rows.at[where, core, at_piece(k)], mate_send.at[where, k], mate_recv.at[where, k], mate)
 
-    def give_copy(where):
-        return remote(parts.at[where, 1 - core], mate_in.at[where], give_send.at[where], give_recv.at[where], mate)
+    def give_copy(where, half):
+        at = at_half(half)
+        return remote(
+            parts.at[where, 1 - core, at], mate_in.at[where, at],
+            give_send.at[where, half], give_recv.at[where, half], mate,
+        )
 
     def sum_copy(where, slot, k, to):
         return remote(
@@ -230,32 +242,25 @@
             shares_ref.at[source], share_in.at[source], share_send.at[source], share_recv.at[source], source
         ).wait_recv()
 
-    def experts_on(where):
-        @pl.loop(0, 2)
-        def _(turn):
-            side = lax.rem(1 - core + turn, 2)
-            block = rows[where, side]
-            gate_part = jnp.dot(block, gate_ref[0], preferred_element_type=jnp.float32)
-            up_part = jnp.dot(block, up_ref[0], preferred_element_type=jnp.float32)
-            act = (gate_part / (1.0 + jnp.exp(-gate_part)) * up_part).astype(jnp.bfloat16)
-            result = jnp.dot(act, down_ref[0], preferred_element_type=jnp.float32)
-            share = share_in[2 * where + side]
-            row_id = lax.broadcasted_iota(jnp.int32, (tok_rows, tok_rows), 0)
-            col_id = lax.broadcasted_iota(jnp.int32, (tok_rows, tok_rows), 1)
-            column = jnp.sum(
-                jnp.where(row_id == col_id, jnp.broadcast_to(share, (tok_rows, tok_rows)), 0.0),
-                axis=1, keepdims=True,
-            )
-            result = result.astype(jnp.bfloat16).astype(jnp.float32)
-            parts[where, side] = (result * column).astype(jnp.bfloat16)
-
-            @pl.when(turn == 0)
-            def _():
-                give_copy(where).start()
-
-
-    def take_rows(where, onward, to):
-        for k in range(CHUNKS):
+    def experts_on(where, half):
+        at = at_half(half)
+        block = jnp.concatenate([rows[where, side, at] for side in range(2)], 0)
+        gate_part = jnp.dot(block, gate_ref[0], preferred_element_type=jnp.float32)
+        up_part = jnp.dot(block, up_ref[0], preferred_element_type=jnp.float32)
+        act = (gate_part / (1.0 + jnp.exp(-gate_part)) * up_part).astype(jnp.bfloat16)
+        result = jnp.dot(act, down_ref[0], preferred_element_type=jnp.float32)
+        row_id = lax.broadcasted_iota(jnp.int32, (half_rows, tok_rows), 0) + half * half_rows
+        col_id = lax.broadcasted_iota(jnp.int32, (half_rows, tok_rows), 1)
+        for side in range(2):
+            share = jnp.broadcast_to(share_in[2 * where + side], (half_rows, tok_rows))
+            column = jnp.sum(jnp.where(row_id == col_id, share, 0.0), axis=1, keepdims=True)
+            mine = result[side * half_rows : (side + 1) * half_rows]
+            mine = mine.astype(jnp.bfloat16).astype(jnp.float32)
+            parts[where, side, at] = (mine * column).astype(jnp.bfloat16)
+        give_copy(where, half).start()
+
+    def take_rows(where, half, onward, to):
+        for k in pieces(half):
             here = rows.at[where, core, at_piece(k)]
             row_copy(here, where, where, k, to).wait_recv()
 
@@ -264,12 +269,12 @@
                 row_copy(here, where, where, k, to).start()
 
             mate_copy(here, where, k).start()
-        for k in range(CHUNKS):
+        for k in pieces(half):
             mate_copy(rows.at[where, core, at_piece(k)], where, k).wait_recv()
 
-    def pass_sum(where, slot_to, more, to):
-        give_copy(where).wait_recv()
-        for k in range(CHUNKS):
+    def pass_sum(where, half, slot_to, more, to):
+        give_copy(where, half).wait_recv()
+        for k in pieces(half):
             at = at_piece(k)
 
             @pl.when(more)
@@ -289,43 +294,47 @@
 
             sum_copy(where, slot_to, k, to).start()
 
-    for k in range(CHUNKS):
-        mate_copy(rows.at[spot, core, at_piece(k)], spot, k).wait_recv()
-    experts_on(spot)
-
-    @pl.loop(1, max(2 * spots - 2, 1))
-    def _(time):
+    @pl.loop(0, HALVES)
+    def _(half):
+        for k in pieces(half):
+            mate_copy(rows.at[spot, core, at_piece(k)], spot, k).wait_recv()
+        experts_on(spot, half)
+
+    @pl.loop(HALVES, max(2 * spots - 2, 1) * HALVES)
+    def _(tick):
+        time, half = tick // HALVES, lax.rem(tick, HALVES)
         low, high = spot - time, spot + time
 
         @pl.when(low >= 0)
         def _():
-            take_rows(low, has_above, jnp.minimum(above, lanes - 2 + core))
+            take_rows(low, half, has_above, jnp.minimum(above, lanes - 2 + core))
 
         @pl.when(high < spots)
         def _():
-            take_rows(high, has_below, jnp.maximum(below, core))
+            take_rows(high, half, has_below, jnp.maximum(below, core))
 
         @pl.when(low >= 0)
         def _():
-            experts_on(low)
+            experts_on(low, half)
 
         @pl.when(high < spots)
         def _():
-            experts_on(high)
+            experts_on(high, half)
 
         down = 2 * spots - 2 - spot - time
 
         @pl.when((down >= 0) & (down < spot))
         def _():
-            pass_sum(down, down, has_above, below)
+            pass_sum(down, half, down, has_above, below)
 
         up = time - spot
 
         @pl.when((up > spot) & (up < spots))
         def _():
-            pass_sum(up, jnp.where(up == spot + 1, spots, up), has_below, above)
-
-    give_copy(spot).wait_recv()
+            pass_sum(up, half, jnp.where(up == spot + 1, spots, up), has_below, above)
+
+    for half in range(HALVES):
+        give_copy(spot, half).wait_recv()
     for k in range(CHUNKS):
         at = at_piece(k)
         out = parts[spot, core, at].astype(jnp.float32) + mate_in[spot, at].astype(jnp.float32)
@@ -376,7 +385,8 @@
 
     @pl.loop(0, spots)
     def _(where):
-        give_copy(where).wait_send()
+        for half in range(HALVES):
+            give_copy(where, half).wait_send()
 
         @pl.when(where != spot)
         def _():
@@ -420,7 +430,7 @@
             dma((lanes,)), dma((lanes,)),
             dma((spots + 1, CHUNKS)), dma((spots, CHUNKS)),
             dma((spots, CHUNKS)), dma((spots, CHUNKS)),
-            dma((spots,)), dma((spots,)),
+            dma((spots, HALVES)), dma((spots, HALVES)),
             dma((spots, CHUNKS)), dma((spots + 1, CHUNKS)),
         ],
         compiler_params=pltpu.CompilerParams(

time: 109 us -> 106 us (0.972); the launches traced: 108 us -> 104 us
  Pallas kernels: 107 us -> 102 us
    pallas_call x1, Pallas kernels: 107 us -> 102 us  [local(): pl.pallas_call(functools.partial(expert_kernel, lanes, total), out_shape=...]
where the time goes in v3:
time: 106 us; the launch traced here: 104 us
  Pallas kernels  102 us (96%)
  local copies, waits for them, and re-layouts  1.87 us (2%)
    pallas_call x1, Pallas kernels, local(): pl.pallas_call(functools.partial(expert_kernel, lanes, total), out_shape=...  102 us

profile of v3, /device:TPU:4, one launch (start us, length us, event | category | flops | bytes accessed | tf_op | source)
XLA Modules:
  0.0 104.3 jit_solution(8613399870000740401)
XLA Ops:
  0.0 102.4 %shard_map.100 = bf16[256,1024]{1,0:T(8,128)(2,1)} custom-call(bf16[256,1024]{1,0:T(8,128)(2,1)} %query_ref.1, bf16[256,512]{1,0:T(8,128)(2,1)} %key_ref.1, bf16[256,512]{1,0:T(8,128)(2,1)} %value_ref.1, bf16[256,1024]{1,0:T(8,128)(2,1)} %residual_ref.1, f32[1,1024]{1,0:T(1,128)} %bitcast.3, s32[2,256]{1,0:T(2,128)} %bitcast.4, f32[2,256]{1,0:T(2,128)} %bitcast.5, ...), custom_call_target="tpu_custom_call" | custom-call | tf_op jit(solution)/shard_map/pallas_call | solution.py:412
  102.4 1.9 %copy.12 = bf16[256,1024]{1,0:T(8,128)(2,1)} copy(bf16[256,1024]{1,0:T(8,128)(2,1)} %shard_map.100) | data formatting | bytes 1048576
